TPU v7x, 256 devices: a whole 4x4x8 slice. The times are simulated.
256 devices in a mesh: ctx: 16 (over y, x), req: 16 (over z, core).
Axes of the slice: x: 4, y: 4, z: 8, core: 2. Of those that a mesh axis runs over, the one named last changes fastest.
Arguments:
- queries: bfloat16 [1024, 64, 128], P('req', 'ctx'), may hold values from -96 to 96
- prefix_keys: bfloat16 [32768, 1024], P('ctx'), may hold values from -9 to 9
- lengths: int32 [64], P('req'), may hold values from 4096 to 32768, as said below
- positions: int32 [64, 16], P('req'), may hold values from 2048 to 34816, as said below
- pool_width: int32 [8], replicated, may hold values from 1 to 7, as said below
- scorer_in: bfloat16 [1024, 1024], replicated, may hold values from -0.1875 to 0.1875
- scorer_out: bfloat16 [1024, 8], replicated, may hold values from -0.1875 to 0.1875
Outputs:
- importance: float32 [8, 32768], P(None, ('ctx', 'req'))
Inputs may be any that keep to these rules, and one draw needn't show every extreme that they name: `lengths`: some request's length is exactly 32768 and some other's exactly 4096. `positions`: each is 2 or more and lies within 2048 of its request's length. `pool_width`: some key head's width is exactly 7 and some other's exactly 1.
All inputs are finite; a program needn't handle non-finite values.
Results may differ from a plain program's by a relative error of at most 0.0003.
The roundings to bfloat16 on the way count: a program that leaves them out, or rounds other values in their place, can miss the bound.
Values may be sent and summed in bfloat16 or wider, within the bound.
No kernel may reach another device: no remote copies, remote signals or barrier semaphores. Data moves between devices by JAX's collectives and lax.ppermute only.
A program may use at most 64 MiB of HBM per device.

v0:
```python
import math

import jax
import jax.numpy as jnp
from jax import lax
from jax.sharding import PartitionSpec as P

RAD = 3


MASKED = -1e30


def joined_along(pieces, dim):
    dims = list(pieces.shape[1:])
    dims[dim] *= pieces.shape[0]
    return jnp.moveaxis(pieces, 0, dim).reshape(dims)


def copy_for_each(array, axis):
    length = lax.axis_size(axis)
    return lax.all_to_all(
        jnp.broadcast_to(array[None], (length, *array.shape)), axis, 0, 0, tiled=True
    )


def gathered_copies(array, axis, dim):
    return joined_along(copy_for_each(array, axis), dim)


def over_copies(array, axis):
    everything = copy_for_each(array, axis)
    return jnp.max(everything, axis=0)


def of_everyone(array, axis):
    everything = copy_for_each(array, axis)
    return jnp.sum(everything, axis=0)


def split_up(array, dim, length):
    dims = array.shape
    pieces = array.reshape(*dims[:dim], length, dims[dim] // length, *dims[dim + 1 :])
    return jnp.moveaxis(pieces, dim, 0)


def sent_and_summed(array, axis, dim):
    length = lax.axis_size(axis)
    pieces = lax.all_to_all(split_up(array, dim, length), axis, 0, 0, tiled=True)
    return jnp.sum(pieces, axis=0)


def with_halo(array, sides, width):
    edges = {}
    for axis, dim in sides:
        size, length = (lax.axis_size(axis), array.shape[dim])
        up = [(i, (i + 1) % size) for i in range(size - 1)]
        last = lax.slice_in_dim(array, length - width, length, axis=dim)
        first = lax.slice_in_dim(array, 0, width, axis=dim)
        edges[dim] = (
            lax.ppermute(last, axis, up),
            lax.ppermute(first, axis, [(b, a) for a, b in up]),
        )
    done = []
    for _, dim in sides:
        low, high = edges[dim]
        around = [(width, width) if d in done else (0, 0) for d in range(array.ndim)]
        array = jnp.concatenate([jnp.pad(low, around), array, jnp.pad(high, around)], axis=dim)
        done.append(dim)
    return array


def block_scores(grouped, key_block, limits, first_key):
    block_width = key_block.shape[0]
    key_heads = grouped.shape[1]
    head_dim = grouped.shape[3]
    keyed_block = key_block.reshape(block_width, key_heads, head_dim)
    products = jnp.einsum(
        "rvgd,kvd->vrgk", grouped, keyed_block, preferred_element_type=jnp.float32
    )
    scaled = products * (1.0 / math.sqrt(head_dim))
    key_index = first_key + lax.iota(jnp.int32, block_width)
    visible = key_index[None, :] <= limits[:, None]
    return jnp.where(visible[None, :, None, :], scaled, MASKED)


def per_device(queries, prefix_keys, lengths, positions, pool_width, scorer_in, scorer_out):
    row_count = queries.shape[0]
    head_dim = queries.shape[2]
    key_heads = pool_width.shape[0]
    key_dev = prefix_keys.shape[0]
    limits = jnp.minimum(positions, lengths[:, None] - 1).reshape(row_count)
    offset = lax.axis_index("ctx") * key_dev
    block_size = 512
    block_count = key_dev // block_size
    gathered = gathered_copies(queries, "ctx", 1)
    held = gathered.reshape(row_count, key_heads, gathered.shape[1] // key_heads, head_dim)

    def fetch_queries():
        return held

    def run_pass(grouped, initial, update):

        def advance(block_index, running):
            first_local = block_index * block_size
            first_key = offset + first_local
            key_block = lax.dynamic_slice_in_dim(prefix_keys, first_local, block_size, 0)
            return update(running, block_scores(grouped, key_block, limits, first_key), first_local)

        return lax.fori_loop(0, block_count, advance, initial)

    group = queries.shape[1] * lax.axis_size("ctx") // key_heads
    stats_shape = (key_heads, row_count, group)
    lowest = jnp.full(stats_shape, MASKED, jnp.float32)
    nothing = jnp.zeros(stats_shape, jnp.float32)

    def max_update(state, scores, first_local):
        return jnp.maximum(state, jnp.max(scores, axis=-1))

    local_max = run_pass(fetch_queries(), lowest, max_update)
    row_max = over_copies(local_max, "ctx")

    def total_update(state, scores, first_local):
        return state + jnp.sum(jnp.exp(scores - row_max[..., None]), axis=-1)

    local_total = run_pass(fetch_queries(), nothing, total_update)
    row_total = of_everyone(local_total, "ctx")

    def accumulate(state, scores, first_local):
        weights = jnp.exp(scores - row_max[..., None]) / row_total[..., None]
        return lax.dynamic_update_slice_in_dim(state, jnp.sum(weights, axis=(1, 2)), first_local, 1)

    columns = run_pass(fetch_queries(), jnp.zeros((key_heads, key_dev), jnp.float32), accumulate)
    owned = sent_and_summed(columns, "req", 1)
    owned_count = owned.shape[1]
    padded = with_halo(owned, ((("ctx", "req"), 1),), RAD)
    window_sum = jnp.zeros_like(owned)
    for tap_offset in range(-RAD, RAD + 1):
        inside = (tap_offset >= -(pool_width // 2)) & (tap_offset <= (pool_width - 1) // 2)
        window_sum = window_sum + jnp.where(
            inside[:, None], padded[:, RAD + tap_offset : RAD + tap_offset + owned_count], 0.0
        )
    pooled = window_sum / pool_width.astype(jnp.float32)[:, None]
    owned_keys = lax.dynamic_slice_in_dim(
        prefix_keys, lax.axis_index("req") * owned_count, owned_count, 0
    )
    hidden = jax.nn.silu(jnp.dot(owned_keys, scorer_in, preferred_element_type=jnp.float32)).astype(
        jnp.bfloat16
    )
    gating = jnp.dot(hidden, scorer_out, preferred_element_type=jnp.float32)
    return pooled * (2.0 * jax.nn.sigmoid(gating.T))


def solution(mesh):
    placed = (P("req", "ctx", None), P("ctx", None), P("req"), P("req", None), P(), P(), P())
    return jax.shard_map(
        per_device, mesh=mesh, in_specs=placed, out_specs=P(None, ("ctx", "req")), check_vma=False
    )
```

profile of v0, /device:TPU:1, one launch (start us, length us, event | category | flops | bytes accessed | tf_op | source)
XLA Modules:
  0.0 143.9 jit_solution(3890115059629447636)
XLA Ops:
  2.3 7.6 %all-to-all-start = ((bf16[16,64,4,128]{3,1,2,0:T(8,128)(2,1)}), bf16[16,64,4,128]{3,1,2,0:T(8,128)(2,1)}, u32[]{:S(2)}, u32[]{:S(2)}) async-start(bf16[16,64,4,128]{3,1,2,0:T(8,128)(2,1)} %broadcast_in_dim.183), calls=%async_computation | async-start | bytes 2097152 | tf_op jit(solution)/shard_map/all_to_all | solution.py:22
  11.4 6.5 %copy.26 = bf16[2048,1024]{0,1:T(8,128)(2,1)} copy(bf16[2048,1024]{1,0:T(8,128)(2,1)} %param.14) | data formatting | bytes 8388608 | tf_op jit(solution)/shard_map/while | solution.py:110
  17.9 8.1 %all-to-all-done = bf16[16,64,4,128]{3,1,2,0:T(8,128)(2,1)} async-done(((bf16[16,64,4,128]{3,1,2,0:T(8,128)(2,1)}), bf16[16,64,4,128]{3,1,2,0:T(8,128)(2,1)}, u32[]{:S(2)}, u32[]{:S(2)}) %all-to-all-start) | async-done | bytes 1048608 | tf_op jit(solution)/shard_map/all_to_all | solution.py:22
  26.0 16.0 %while.45 = (s32[]{:T(128)}, f32[8,64,8]{1,2,0:T(8,128)S(1)}, s32[]{:T(128)}, s32[4,16]{1,0:T(4,128)}, bf16[2048,1024]{0,1:T(8,128)(2,1)}, /*index=5*/bf16[64,8,...) while((s32[]{:T(128)}, f32[8,64,8]{1,2,0:T(8,128)S(1)}, ...), condition=%wide.wide.region_2.3_spmd.clone, body=%wide.wide.region_0.2_spmd.clone.sunk | while | flops 543199744 | bytes 4329913 | solution.py:110
  27.4 2.5 %fusion.76 = f32[8,64,8]{1,2,0:T(8,128)S(1)} fusion(pred[64,512]{1,0:T(8,128)(4,1)S(1)} %broadcast_compare_fusion.10, bf16[512,8,128,1]{0,2,3,1:T(8,128)(2,1)S(1)} %bitcast.99, bf16[64,8,8,128]{3,0,2,1:T(8,128)(2,1)} %get-tuple-element.778), kind=kOutput, calls=%fused_computation.10.clone.clone.1 | convolution fusion | flops 543158272 | bytes 2146304 | tf_op jit(solution)/shard_map/while/body/eval_jaxpr/rvgd,kvd->vrgk/dot_general | solution.py:78
  31.4 2.5 %fusion.76 = f32[8,64,8]{1,2,0:T(8,128)S(1)} fusion(pred[64,512]{1,0:T(8,128)(4,1)S(1)} %broadcast_compare_fusion.10, bf16[512,8,128,1]{0,2,3,1:T(8,128)(2,1)S(1)} %bitcast.99, bf16[64,8,8,128]{3,0,2,1:T(8,128)(2,1)} %get-tuple-element.778), kind=kOutput, calls=%fused_computation.10.clone.clone.1 | convolution fusion | flops 543158272 | bytes 2146304 | tf_op jit(solution)/shard_map/while/body/eval_jaxpr/rvgd,kvd->vrgk/dot_general | solution.py:78
  35.4 2.5 %fusion.76 = f32[8,64,8]{1,2,0:T(8,128)S(1)} fusion(pred[64,512]{1,0:T(8,128)(4,1)S(1)} %broadcast_compare_fusion.10, bf16[512,8,128,1]{0,2,3,1:T(8,128)(2,1)S(1)} %bitcast.99, bf16[64,8,8,128]{3,0,2,1:T(8,128)(2,1)} %get-tuple-element.778), kind=kOutput, calls=%fused_computation.10.clone.clone.1 | convolution fusion | flops 543158272 | bytes 2146304 | tf_op jit(solution)/shard_map/while/body/eval_jaxpr/rvgd,kvd->vrgk/dot_general | solution.py:78
  43.1 4.2 %all-to-all-start.1 = ((f32[16,1,4096]{2,1,0:T(1,128)}), f32[16,1,4096]{2,1,0:T(1,128)S(1)}, u32[]{:S(2)}, u32[]{:S(2)}) async-start(f32[16,1,4096]{2,1,0:T(1,128)} %reshape.157), calls=%async_computation.1 | async-start | bytes 524288 | tf_op jit(solution)/shard_map/all_to_all | solution.py:22
  48.0 6.8 %all-to-all-done.1 = f32[16,1,4096]{2,1,0:T(1,128)S(1)} async-done(((f32[16,1,4096]{2,1,0:T(1,128)}), f32[16,1,4096]{2,1,0:T(1,128)S(1)}, u32[]{:S(2)}, u32[]{:S(2)}) %all-to-all-start.1) | async-done | bytes 262176 | tf_op jit(solution)/shard_map/all_to_all | solution.py:22
  56.8 20.4 %while.46 = (s32[]{:T(128)}, f32[8,64,8]{1,2,0:T(8,128)S(1)}, s32[]{:T(128)}, s32[4,16]{1,0:T(4,128)}, bf16[2048,1024]{0,1:T(8,128)(2,1)}, /*index=5*/bf16[64,8,...) while((s32[]{:T(128)}, f32[8,64,8]{1,2,0:T(8,128)S(1)}, ...), condition=%wide.wide.region_6.7_spmd.clone, body=%wide.wide.region_4.6_spmd.clone.sunk | while | flops 545296896 | bytes 4346305 | solution.py:110
  58.2 3.6 %fusion.79 = f32[8,64,8]{1,2,0:T(8,128)S(1)} fusion(f32[8,64,8]{1,2,0:T(8,128)S(1)} %get-tuple-element.814, pred[64,512]{1,0:T(8,128)(4,1)S(1)} %broadcast_compare_fusion.11, bf16[512,8,128,1]{0,2,3,1:T(8,128)(2,1)S(1)} %bitcast.100, bf16[64,8,8,128]{3,0,2,1:T(8,128)(2,1)} %get-tuple-element.813), kind=kOutput, calls=%fused_computation.18.clone.clone.1 | convolution fusion | flops 545255424 | bytes 2162688 | tf_op jit(solution)/shard_map/while/body/eval_jaxpr/rvgd,kvd->vrgk/dot_general | solution.py:78
  63.3 3.6 %fusion.79 = f32[8,64,8]{1,2,0:T(8,128)S(1)} fusion(f32[8,64,8]{1,2,0:T(8,128)S(1)} %get-tuple-element.814, pred[64,512]{1,0:T(8,128)(4,1)S(1)} %broadcast_compare_fusion.11, bf16[512,8,128,1]{0,2,3,1:T(8,128)(2,1)S(1)} %bitcast.100, bf16[64,8,8,128]{3,0,2,1:T(8,128)(2,1)} %get-tuple-element.813), kind=kOutput, calls=%fused_computation.18.clone.clone.1 | convolution fusion | flops 545255424 | bytes 2162688 | tf_op jit(solution)/shard_map/while/body/eval_jaxpr/rvgd,kvd->vrgk/dot_general | solution.py:78
  68.4 3.7 %fusion.79 = f32[8,64,8]{1,2,0:T(8,128)S(1)} fusion(f32[8,64,8]{1,2,0:T(8,128)S(1)} %get-tuple-element.814, pred[64,512]{1,0:T(8,128)(4,1)S(1)} %broadcast_compare_fusion.11, bf16[512,8,128,1]{0,2,3,1:T(8,128)(2,1)S(1)} %bitcast.100, bf16[64,8,8,128]{3,0,2,1:T(8,128)(2,1)} %get-tuple-element.813), kind=kOutput, calls=%fused_computation.18.clone.clone.1 | convolution fusion | flops 545255424 | bytes 2162688 | tf_op jit(solution)/shard_map/while/body/eval_jaxpr/rvgd,kvd->vrgk/dot_general | solution.py:78
  73.5 3.6 %fusion.79 = f32[8,64,8]{1,2,0:T(8,128)S(1)} fusion(f32[8,64,8]{1,2,0:T(8,128)S(1)} %get-tuple-element.814, pred[64,512]{1,0:T(8,128)(4,1)S(1)} %broadcast_compare_fusion.11, bf16[512,8,128,1]{0,2,3,1:T(8,128)(2,1)S(1)} %bitcast.100, bf16[64,8,8,128]{3,0,2,1:T(8,128)(2,1)} %get-tuple-element.813), kind=kOutput, calls=%fused_computation.18.clone.clone.1 | convolution fusion | flops 545255424 | bytes 2162688 | tf_op jit(solution)/shard_map/while/body/eval_jaxpr/rvgd,kvd->vrgk/dot_general | solution.py:78
  78.3 3.5 %all-to-all-start.2 = ((f32[16,1,4096]{2,1,0:T(1,128)}), f32[16,1,4096]{2,1,0:T(1,128)S(1)}, u32[]{:S(2)}, u32[]{:S(2)}) async-start(f32[16,1,4096]{2,1,0:T(1,128)} %reshape.159), calls=%async_computation.2 | async-start | bytes 524288 | tf_op jit(solution)/shard_map/all_to_all | solution.py:22
  82.6 6.7 %all-to-all-done.2 = f32[16,1,4096]{2,1,0:T(1,128)S(1)} async-done(((f32[16,1,4096]{2,1,0:T(1,128)}), f32[16,1,4096]{2,1,0:T(1,128)S(1)}, u32[]{:S(2)}, u32[]{:S(2)}) %all-to-all-start.2) | async-done | bytes 262176 | tf_op jit(solution)/shard_map/all_to_all | solution.py:22
  91.4 22.7 %while.44 = (s32[]{:T(128)}, f32[8,2048]{1,0:T(8,128)}, s32[]{:T(128)}, s32[4,16]{1,0:T(4,128)}, bf16[2048,1024]{0,1:T(8,128)(2,1)}, /*index=5*/bf16[64,8,8,128]...) while((s32[]{:T(128)}, f32[8,2048]{1,0:T(8,128)}, ...), condition=%wide.wide.region_10.11_spmd, body=%wide.wide.region_8.10_spmd.sunk | while | flops 547385856 | bytes 4346307 | solution.py:110
  92.8 3.6 %fusion.73 = f32[8,512]{1,0:T(8,128)S(1)} fusion(f32[8,64,8]{1,2,0:T(8,128)S(1)} %get-tuple-element.853, f32[8,64,8]{1,2,0:T(8,128)S(1)} %get-tuple-element.852, pred[64,512]{1,0:T(8,128)(4,1)S(1)} %broadcast_compare_fusion.9, bf16[512,8,128,1]{0,2,3,1:T(8,128)(2,1)S(1)} %bitcast.101, bf16[64,8,8,128]{3,0,2,1:T(8,128)(2,1)} %get-tuple-element.851), kind=kOutput, calls=%fused_computation.4.clone.clone.1 | convolution fusion | flops 547352576 | bytes 2179072 | tf_op jit(solution)/shard_map/while/body/eval_jaxpr/rvgd,kvd->vrgk/dot_general | solution.py:78
  98.5 3.6 %fusion.73 = f32[8,512]{1,0:T(8,128)S(1)} fusion(f32[8,64,8]{1,2,0:T(8,128)S(1)} %get-tuple-element.853, f32[8,64,8]{1,2,0:T(8,128)S(1)} %get-tuple-element.852, pred[64,512]{1,0:T(8,128)(4,1)S(1)} %broadcast_compare_fusion.9, bf16[512,8,128,1]{0,2,3,1:T(8,128)(2,1)S(1)} %bitcast.101, bf16[64,8,8,128]{3,0,2,1:T(8,128)(2,1)} %get-tuple-element.851), kind=kOutput, calls=%fused_computation.4.clone.clone.1 | convolution fusion | flops 547352576 | bytes 2179072 | tf_op jit(solution)/shard_map/while/body/eval_jaxpr/rvgd,kvd->vrgk/dot_general | solution.py:78
  104.2 3.6 %fusion.73 = f32[8,512]{1,0:T(8,128)S(1)} fusion(f32[8,64,8]{1,2,0:T(8,128)S(1)} %get-tuple-element.853, f32[8,64,8]{1,2,0:T(8,128)S(1)} %get-tuple-element.852, pred[64,512]{1,0:T(8,128)(4,1)S(1)} %broadcast_compare_fusion.9, bf16[512,8,128,1]{0,2,3,1:T(8,128)(2,1)S(1)} %bitcast.101, bf16[64,8,8,128]{3,0,2,1:T(8,128)(2,1)} %get-tuple-element.851), kind=kOutput, calls=%fused_computation.4.clone.clone.1 | convolution fusion | flops 547352576 | bytes 2179072 | tf_op jit(solution)/shard_map/while/body/eval_jaxpr/rvgd,kvd->vrgk/dot_general | solution.py:78
  109.8 3.6 %fusion.73 = f32[8,512]{1,0:T(8,128)S(1)} fusion(f32[8,64,8]{1,2,0:T(8,128)S(1)} %get-tuple-element.853, f32[8,64,8]{1,2,0:T(8,128)S(1)} %get-tuple-element.852, pred[64,512]{1,0:T(8,128)(4,1)S(1)} %broadcast_compare_fusion.9, bf16[512,8,128,1]{0,2,3,1:T(8,128)(2,1)S(1)} %bitcast.101, bf16[64,8,8,128]{3,0,2,1:T(8,128)(2,1)} %get-tuple-element.851), kind=kOutput, calls=%fused_computation.4.clone.clone.1 | convolution fusion | flops 547352576 | bytes 2179072 | tf_op jit(solution)/shard_map/while/body/eval_jaxpr/rvgd,kvd->vrgk/dot_general | solution.py:78
  114.1 12.6 %all-to-all-start.3 = ((f32[16,8,128]{2,1,0:T(8,128)}), f32[16,8,128]{2,1,0:T(8,128)S(1)}, u32[]{:S(2)}, u32[]{:S(2)}) async-start(f32[16,8,128]{2,1,0:T(8,128)} %bitcast.7), calls=%async_computation.3 | async-start | bytes 131072 | tf_op jit(solution)/shard_map/all_to_all | solution.py:49
  126.7 7.8 %all-to-all-done.3 = f32[16,8,128]{2,1,0:T(8,128)S(1)} async-done(((f32[16,8,128]{2,1,0:T(8,128)}), f32[16,8,128]{2,1,0:T(8,128)S(1)}, u32[]{:S(2)}, u32[]{:S(2)}) %all-to-all-start.3) | async-done | bytes 65568 | tf_op jit(solution)/shard_map/all_to_all | solution.py:49
  138.9 2.9 %collective-permute-done.1 = f32[8,3]{1,0:T(8,128)S(1)} collective-permute-done((f32[8,3]{1,0:T(8,128)S(1)}, f32[8,3]{1,0:T(8,128)S(1)}, u32[]{:S(2)}, u32[]{:S(2)}) %collective-permute-start.1) | collective-permute-done | bytes 128 | tf_op jit(solution)/shard_map/ppermute | solution.py:62
  (87 shorter events, 39.7 us)
Async XLA Ops:
  0.0 141.8 %copy-start = (bf16[1024,1024]{1,0:T(8,128)(2,1)S(1)}, bf16[1024,1024]{1,0:T(8,128)(2,1)}, u32[]{:S(2)}) copy-start(bf16[1024,1024]{1,0:T(8,128)(2,1)} %param.18) | copy-start | bytes 6291460
  2.3 23.7 %all-to-all-start = ((bf16[16,64,4,128]{3,1,2,0:T(8,128)(2,1)}), bf16[16,64,4,128]{3,1,2,0:T(8,128)(2,1)}, u32[]{:S(2)}, u32[]{:S(2)}) async-start(bf16[16,64,4,128]{3,1,2,0:T(8,128)(2,1)} %broadcast_in_dim.183), calls=%async_computation | async-start | bytes 2097152 | tf_op jit(solution)/shard_map/all_to_all | solution.py:22
  11.3 6.6 %copy-start.1 = (s32[4,16]{1,0:T(4,128)}, s32[4,16]{1,0:T(4,128)S(1)}, u32[]{:S(2)}) copy-start(s32[4,16]{1,0:T(4,128)S(1)} %broadcast_minimum_fusion) | copy-start | bytes 772
  43.1 11.8 %all-to-all-start.1 = ((f32[16,1,4096]{2,1,0:T(1,128)}), f32[16,1,4096]{2,1,0:T(1,128)S(1)}, u32[]{:S(2)}, u32[]{:S(2)}) async-start(f32[16,1,4096]{2,1,0:T(1,128)} %reshape.157), calls=%async_computation.1 | async-start | bytes 524288 | tf_op jit(solution)/shard_map/all_to_all | solution.py:22
  56.8 25.8 %copy-start.2 = (s32[8]{0:T(128)S(1)}, s32[8]{0:T(128)}, u32[]{:S(2)}) copy-start(s32[8]{0:T(128)} %param.17) | copy-start | bytes 100
  78.3 11.0 %all-to-all-start.2 = ((f32[16,1,4096]{2,1,0:T(1,128)}), f32[16,1,4096]{2,1,0:T(1,128)S(1)}, u32[]{:S(2)}, u32[]{:S(2)}) async-start(f32[16,1,4096]{2,1,0:T(1,128)} %reshape.159), calls=%async_computation.2 | async-start | bytes 524288 | tf_op jit(solution)/shard_map/all_to_all | solution.py:22
  91.4 50.3 %copy-start.3 = (bf16[1024,8]{0,1:T(8,128)(2,1)S(1)}, bf16[1024,8]{0,1:T(8,128)(2,1)}, u32[]{:S(2)}) copy-start(bf16[1024,8]{0,1:T(8,128)(2,1)} %param.19) | copy-start | bytes 49156
  114.1 20.4 %all-to-all-start.3 = ((f32[16,8,128]{2,1,0:T(8,128)}), f32[16,8,128]{2,1,0:T(8,128)S(1)}, u32[]{:S(2)}, u32[]{:S(2)}) async-start(f32[16,8,128]{2,1,0:T(8,128)} %bitcast.7), calls=%async_computation.3 | async-start | bytes 131072 | tf_op jit(solution)/shard_map/all_to_all | solution.py:49
  134.6 4.3 %collective-permute-start = (f32[8,3]{1,0:T(8,128)S(1)}, f32[8,3]{1,0:T(8,128)S(1)}, u32[]{:S(2)}, u32[]{:S(2)}) collective-permute-start(f32[8,3]{1,0:T(8,128)S(1)} %get-tuple-element.512), channel_id=1, source_target_pairs={{0,1},{1,2},{2,3},{3,4},{4,5},{5,6},{6,7},{7,8},{8,9},{9,10},{10,1... | collective-permute-start | bytes 296 | tf_op jit(solution)/shard_map/ppermute | solution.py:61
  136.8 4.9 %collective-permute-start.1 = (f32[8,3]{1,0:T(8,128)S(1)}, f32[8,3]{1,0:T(8,128)S(1)}, u32[]{:S(2)}, u32[]{:S(2)}) collective-permute-start(f32[8,3]{1,0:T(8,128)S(1)} %get-tuple-element.513), channel_id=1, source_target_pairs={{1,0},{2,1},{3,2},{4,3},{5,4},{6,5},{7,6},{8,7},{9,8},{10,9},{11,1... | collective-permute-start | bytes 296 | tf_op jit(solution)/shard_map/ppermute | solution.py:62
where the time goes:
time: 146 us; the launch traced here: 144 us
  matrix products  41.5 us (28%)
  starting transfers between devices  32.3 us (22%)
  local copies, waits for them, and re-layouts  32.2 us (22%)
  waiting for transfers between devices  32.2 us (22%)
  other arithmetic  5 us (3%)
    dot_general x12, matrix products, block_scores(): jnp.einsum('rvgd,kvd->vrgk', grouped, keyed_block, preferred_element_type...  39.4 us
    all_to_all x3, waiting for transfers between devices, copy_for_each(): lax.all_to_all(jnp.broadcast_to(array[None], (length, *array.shape)), axi...  21.6 us
    dynamic_slice x12, local copies, waits for them, and re-layouts, advance(): lax.dynamic_slice_in_dim(prefix_keys, first_local, block_size, 0)  15.6 us
    all_to_all x3, starting transfers between devices, copy_for_each(): lax.all_to_all(jnp.broadcast_to(array[None], (length, *array.shape)), axi...  15.4 us
    all_to_all x1, starting transfers between devices, sent_and_summed(): lax.all_to_all(split_up(array, dim, length), axis, 0, 0, tiled=True)  12.6 us
    all_to_all x1, waiting for transfers between devices, sent_and_summed(): lax.all_to_all(split_up(array, dim, length), axis, 0, 0, tiled=True)  7.76 us
    while x1, local copies, waits for them, and re-layouts, run_pass(): return lax.fori_loop(0, block_count, advance, initial)  6.49 us
    unnamed x15, local copies, waits for them, and re-layouts  3.6 us
  transfers between devices with their start and end apart: 6, of which 5 were waited for; matrix products, arithmetic and copies ran while one was open for 7% of the time, Pallas kernels for 0%

commit v1 on v0

v1 whole, which is shorter than its diff:
```python
import math

import jax
import jax.numpy as jnp
from jax import lax
from jax.experimental import pallas as pl
from jax.experimental.pallas import tpu as pltpu
from jax.sharding import PartitionSpec as P

RAD = 3
MASKED = -1e30
LOG2E = 1.4426950408889634
HALO = 128
EDGE = 16
NT = (((1,), (1,)), ((), ()))


def penalty_rows(first_key, count, limits, is_halo, key_total, key_dev):
    local = lax.broadcasted_iota(jnp.int32, (count, 128), 0)
    if is_halo:
        after = local < HALO // 2
        key = jnp.where(after, first_key + key_dev + local, first_key - HALO + local)
        real = ((local < RAD) | (local >= HALO - RAD)) & (key >= 0) & (key < key_total)
        return jnp.where(real & (key <= limits), 0.0, MASKED).astype(jnp.bfloat16)
    return jnp.where(first_key + local <= limits, 0.0, MASKED).astype(jnp.bfloat16)


def one_hot_rows(chunk_rows, heads, row_count):
    row = lax.broadcasted_iota(jnp.int32, (chunk_rows, 128), 0)
    lane = lax.broadcasted_iota(jnp.int32, (chunk_rows, 128), 1)
    low = lane * heads
    return jnp.where((row >= low) & (row < low + heads), 1.0, 0.0).astype(jnp.bfloat16)


def stats_kernel(first_ref, q_ref, k_ref, lim_ref, out_ref, kaug, qaug, lse, *, heads, row_count, scale2):
    v = pl.program_id(0)
    per, chunk_rows, head_dim = q_ref.shape
    key_dev = k_ref.shape[0]
    block = 256

    @pl.when(v == 0)
    def _():
        for b in range(key_dev // block):
            kaug[b * block : (b + 1) * block, head_dim:] = penalty_rows(
                first_ref[0] + b * block, block, lim_ref[...], False, 0, 0
            )
        hot = one_hot_rows(chunk_rows, heads, row_count)
        for p in range(per):
            qaug[p * chunk_rows : (p + 1) * chunk_rows, head_dim:] = hot

    kaug[:, :head_dim] = k_ref[...]
    for p in range(per):
        qaug[p * chunk_rows : (p + 1) * chunk_rows, :head_dim] = q_ref[p]
    for p in range(per):
        s = lax.dot_general(
            kaug[...], qaug[p * chunk_rows : (p + 1) * chunk_rows], NT, preferred_element_type=jnp.float32
        )
        top = jnp.max(s, axis=0, keepdims=True) * scale2
        total = jnp.sum(jnp.exp2(s * scale2 - top), axis=0, keepdims=True)
        lse[pl.ds(v * per + p, 1), :] = top + jnp.log2(total)

    @pl.when(v == pl.num_programs(0) - 1)
    def _():
        everything = lse[...]
        for i in range(out_ref.shape[0]):
            out_ref[i] = everything


def to_column(row):
    r = lax.broadcasted_iota(jnp.int32, (128, 128), 0)
    c = lax.broadcasted_iota(jnp.int32, (128, 128), 1)
    return jnp.sum(jnp.where(r == c, row, 0.0), axis=1, keepdims=True)


def columns_kernel(
    first_ref, q_ref, k_ref, next_ref, prev_ref, lim_ref, parts_ref, width_ref, out_ref,
    kaug, qaug, lse, cols, *, heads, row_count, scale2, key_total,
):
    v = pl.program_id(0)
    per, chunk_rows, head_dim = q_ref.shape
    key_dev = k_ref.shape[0]
    block = 256

    @pl.when(v == 0)
    def _():
        for b in range(key_dev // block):
            kaug[b * block : (b + 1) * block, head_dim:] = penalty_rows(
                first_ref[0] + b * block, block, lim_ref[...], False, 0, 0
            )
        kaug[key_dev:, head_dim:] = penalty_rows(first_ref[0], HALO, lim_ref[...], True, key_total, key_dev)
        kaug[key_dev:, :head_dim] = jnp.zeros((HALO, head_dim), jnp.bfloat16)
        hot = one_hot_rows(chunk_rows, heads, row_count)
        for p in range(per):
            qaug[p * chunk_rows : (p + 1) * chunk_rows, head_dim:] = hot
        peers = parts_ref.shape[0]
        top = parts_ref[0]
        for i in range(1, peers):
            top = jnp.maximum(top, parts_ref[i])
        total = jnp.exp2(parts_ref[0] - top)
        for i in range(1, peers):
            total = total + jnp.exp2(parts_ref[i] - top)
        lse[...] = top + jnp.log2(total)

    kaug[:key_dev, :head_dim] = k_ref[...]
    kaug[key_dev : key_dev + EDGE, :head_dim] = next_ref[...]
    kaug[key_dev + HALO - EDGE :, :head_dim] = prev_ref[...]
    for p in range(per):
        qaug[p * chunk_rows : (p + 1) * chunk_rows, :head_dim] = q_ref[p]
    columns = []
    for p in range(per):
        row = lse[pl.ds(v * per + p, 1), :]
        for j in range(chunk_rows // 128):
            columns.append(to_column(row[:, j * 128 : (j + 1) * 128]))
    shift = jnp.concatenate(columns, axis=0)
    start = 0
    while start < key_dev + HALO:
        size = min(block, key_dev + HALO - start)
        s = lax.dot_general(qaug[...], kaug[start : start + size], NT, preferred_element_type=jnp.float32)
        weights = jnp.exp2(s * scale2 - shift)
        cols[v, :, start : start + size] = jnp.sum(weights.reshape(-1, 8, size), axis=0)
        start += size

    @pl.when(v == pl.num_programs(0) - 1)
    def _():
        width = width_ref[...]
        below = width // 2
        above = (width - 1) // 2
        whole = jnp.sum(cols[...], axis=1)
        length = whole.shape[1]
        pooled = jnp.where(above >= 0, whole, 0.0)
        for tap in range(1, RAD + 1):
            pooled = pooled + jnp.where(tap <= above, pltpu.roll(whole, length - tap, 1), 0.0)
            pooled = pooled + jnp.where(tap <= below, pltpu.roll(whole, tap, 1), 0.0)
        pooled = pooled / width.astype(jnp.float32)
        piece = key_dev // out_ref.shape[0]
        for i in range(out_ref.shape[0]):
            out_ref[i] = pooled[:, i * piece : (i + 1) * piece]


def row_stats(first, chunks, keys, lim, key_heads, heads, scale2):
    n, chunk_rows, head_dim = chunks.shape
    per = n // key_heads
    key_dev = keys.shape[0]
    return pl.pallas_call(
        lambda *refs: stats_kernel(*refs, heads=heads, row_count=chunk_rows // heads, scale2=scale2),
        out_shape=jax.ShapeDtypeStruct((n, n, chunk_rows), jnp.float32),
        grid=(key_heads,),
        in_specs=[
            pl.BlockSpec(memory_space=pltpu.SMEM),
            pl.BlockSpec((per, chunk_rows, head_dim), lambda v: (v, 0, 0)),
            pl.BlockSpec((key_dev, head_dim), lambda v: (0, v)),
            pl.BlockSpec((1, 128), lambda v: (0, 0)),
        ],
        out_specs=pl.BlockSpec((n, n, chunk_rows), lambda v: (0, 0, 0)),
        scratch_shapes=[
            pltpu.VMEM((key_dev, 2 * head_dim), jnp.bfloat16),
            pltpu.VMEM((per * chunk_rows, 2 * head_dim), jnp.bfloat16),
            pltpu.VMEM((n, chunk_rows), jnp.float32),
        ],
        name="row_stats",
    )(first, chunks, keys, lim)


def key_columns(first, chunks, keys, after, before, lim, parts, width, key_heads, heads, scale2, key_total, owners):
    n, chunk_rows, head_dim = chunks.shape
    per = n // key_heads
    key_dev = keys.shape[0]
    return pl.pallas_call(
        lambda *refs: columns_kernel(
            *refs, heads=heads, row_count=chunk_rows // heads, scale2=scale2, key_total=key_total
        ),
        out_shape=jax.ShapeDtypeStruct((owners, key_heads, key_dev // owners), jnp.float32),
        grid=(key_heads,),
        in_specs=[
            pl.BlockSpec(memory_space=pltpu.SMEM),
            pl.BlockSpec((per, chunk_rows, head_dim), lambda v: (v, 0, 0)),
            pl.BlockSpec((key_dev, head_dim), lambda v: (0, v)),
            pl.BlockSpec((EDGE, head_dim), lambda v: (0, v)),
            pl.BlockSpec((EDGE, head_dim), lambda v: (0, v)),
            pl.BlockSpec((1, 128), lambda v: (0, 0)),
            pl.BlockSpec((n, n, chunk_rows), lambda v: (0, 0, 0)),
            pl.BlockSpec((key_heads, 1), lambda v: (0, 0)),
        ],
        out_specs=pl.BlockSpec((owners, key_heads, key_dev // owners), lambda v: (0, 0, 0)),
        scratch_shapes=[
            pltpu.VMEM((key_dev + HALO, 2 * head_dim), jnp.bfloat16),
            pltpu.VMEM((per * chunk_rows, 2 * head_dim), jnp.bfloat16),
            pltpu.VMEM((n, chunk_rows), jnp.float32),
            pltpu.VMEM((key_heads, 8, key_dev + HALO), jnp.float32),
        ],
        name="key_columns",
    )(first, chunks, keys, after, before, lim, parts, width)


def sent_to_all(array, axis):
    length = lax.axis_size(axis)
    return lax.all_to_all(jnp.broadcast_to(array[None], (length, *array.shape)), axis, 0, 0, tiled=True)


def per_device(queries, prefix_keys, lengths, positions, pool_width, scorer_in, scorer_out):
    row_count, heads, head_dim = queries.shape
    key_heads = pool_width.shape[0]
    key_dev = prefix_keys.shape[0]
    shards = lax.axis_size("ctx")
    owners = lax.axis_size("req")
    scale2 = LOG2E / math.sqrt(head_dim)
    limits = jnp.minimum(positions, lengths[:, None] - 1).reshape(1, row_count)
    lim = jnp.pad(limits, ((0, 0), (0, 128 - row_count)), constant_values=2**30)
    first = (lax.axis_index("ctx") * key_dev).reshape(1).astype(jnp.int32)
    up = [(i, i + 1) for i in range(shards - 1)]
    chunks = sent_to_all(queries.reshape(row_count * heads, head_dim), "ctx")
    chunks = chunks.reshape(shards, row_count * heads, head_dim)
    before = lax.ppermute(prefix_keys[key_dev - EDGE :], "ctx", up)
    after = lax.ppermute(prefix_keys[:EDGE], "ctx", [(b, a) for a, b in up])

    owned = key_dev // owners
    owned_keys = lax.dynamic_slice_in_dim(prefix_keys, lax.axis_index("req") * owned, owned, 0)
    hidden = jax.nn.silu(jnp.dot(owned_keys, scorer_in, preferred_element_type=jnp.float32)).astype(jnp.bfloat16)
    gating = jnp.dot(hidden, scorer_out, preferred_element_type=jnp.float32)
    gate = (2.0 * jax.nn.sigmoid(gating)).T
    chunks, gate, before, after = lax.optimization_barrier((chunks, gate, before, after))

    local = row_stats(first, chunks, prefix_keys, lim, key_heads, heads, scale2)
    parts = lax.all_to_all(local, "ctx", 0, 0, tiled=True)
    pooled = key_columns(
        first, chunks, prefix_keys, after, before, lim, parts, pool_width.reshape(key_heads, 1),
        key_heads, heads, scale2, shards * key_dev, owners,
    )
    pieces = lax.all_to_all(pooled, "req", 0, 0, tiled=True)
    return jnp.sum(pieces, axis=0) * gate


def solution(mesh):
    placed = (P("req", "ctx", None), P("ctx", None), P("req"), P("req", None), P(), P(), P())
    return jax.shard_map(
        per_device, mesh=mesh, in_specs=placed, out_specs=P(None, ("ctx", "req")), check_vma=False
    )
```

time: 146 us -> 83.8 us (0.57)
  matrix products: 41.5 us -> 1.54 us
  local copies, waits for them, and re-layouts: 32.2 us -> 6.01 us
  Pallas kernels: 0 us -> 24.1 us
  blocking collectives: 0 us -> 18.4 us
  waiting for transfers between devices: 32.2 us -> 14.5 us
  starting transfers between devices: 32.3 us -> 17.1 us
  other arithmetic: 5 us -> 1.38 us
    dot_general x12 -> x0, matrix products: 39.4 us -> none  [block_scores(): jnp.einsum('rvgd,kvd->vrgk', grouped, keyed_block, preferred_element_type...]
    pallas_call x0 -> x2, Pallas kernels: none -> 24.1 us  [the longest x1 13.7 us: row_stats(): pl.pallas_call(lambda *refs: stats_kernel(*refs, heads=heads, row_count=c...]
    all_to_all x4 -> x2, waiting for transfers between devices: 29.4 us -> 9.48 us  [the longest x1 6.86 us: per_device(): parts = lax.all_to_all(local, 'ctx', 0, 0, tiled=True)]
    all_to_all x0 -> x1, blocking collectives: none -> 18.4 us  [per_device(): pieces = lax.all_to_all(pooled, 'req', 0, 0, tiled=True)]
    dynamic_slice x12 -> x0, local copies, waits for them, and re-layouts: 15.6 us -> none  [advance(): lax.dynamic_slice_in_dim(prefix_keys, first_local, block_size, 0)]
    all_to_all x4 -> x2, starting transfers between devices: 28 us -> 12.6 us  [the longest x1 7.57 us: sent_to_all(): lax.all_to_all(jnp.broadcast_to(array[None], (length, *array.shape)), axi...]
    while x1 -> x0, local copies, waits for them, and re-layouts: 6.49 us -> none  [run_pass(): return lax.fori_loop(0, block_count, advance, initial)]
    dynamic_update_slice x4 -> x0, local copies, waits for them, and re-layouts: 2.43 us -> none  [accumulate(): lax.dynamic_update_slice_in_dim(state, jnp.sum(weights, axis=(1, 2)), fir...]
  transfers between devices with their start and end apart: 6 -> 4, of which waited for: 5 -> 4; matrix products, arithmetic and copies ran while one was open for 7% -> 5% of each run, Pallas kernels for 0% -> 0%
where the time goes in v1:
time: 83.8 us; the launch traced here: 83.2 us
  Pallas kernels  24.1 us (29%)
  blocking collectives  18.4 us (22%)
  starting transfers between devices  17.1 us (20%)
  waiting for transfers between devices  14.5 us (17%)
  local copies, waits for them, and re-layouts  6.01 us (7%)
  matrix products  1.54 us (2%)
  other arithmetic  1.38 us (2%)
    all_to_all x1, blocking collectives, per_device(): pieces = lax.all_to_all(pooled, 'req', 0, 0, tiled=True)  18.4 us
    pallas_call x1, Pallas kernels, row_stats(): pl.pallas_call(lambda *refs: stats_kernel(*refs, heads=heads, row_count=c...  13.7 us
    pallas_call x1, Pallas kernels, key_columns(): pl.pallas_call(lambda *refs: columns_kernel(*refs, heads=heads, row_count...  10.3 us
    all_to_all x1, starting transfers between devices, sent_to_all(): lax.all_to_all(jnp.broadcast_to(array[None], (length, *array.shape)), axi...  7.57 us
    all_to_all x1, waiting for transfers between devices, per_device(): parts = lax.all_to_all(local, 'ctx', 0, 0, tiled=True)  6.86 us
    all_to_all x1, starting transfers between devices, per_device(): parts = lax.all_to_all(local, 'ctx', 0, 0, tiled=True)  5.03 us
    ppermute x1, starting transfers between devices, per_device(): before = lax.ppermute(prefix_keys[key_dev - EDGE:], 'ctx', up)  3.26 us
    ppermute x1, waiting for transfers between devices, per_device(): before = lax.ppermute(prefix_keys[key_dev - EDGE:], 'ctx', up)  3.09 us
  transfers between devices with their start and end apart: 4, of which 4 were waited for; matrix products, arithmetic and copies ran while one was open for 5% of the time, Pallas kernels for 0%

profile of v1, /device:TPU:1, one launch (start us, length us, event | category | flops | bytes accessed | tf_op | source)
XLA Modules:
  0.0 83.2 jit_solution(12969679574614643278)
XLA Ops:
  0.0 0.0 copy-start
  0.0 2.2 %broadcast_in_dim.9 = bf16[16,256,128]{2,1,0:T(8,128)(2,1)} broadcast(bf16[256,128]{1,0:T(8,128)(2,1)} %bitcast.7), dimensions={1,2} | broadcast | bytes 1114112 | tf_op jit(solution)/shard_map/broadcast_in_dim | solution.py:197
  2.2 7.6 %all-to-all-start = ((bf16[16,256,128]{2,1,0:T(8,128)(2,1)}), bf16[16,256,128]{2,1,0:T(8,128)(2,1)S(1)}, u32[]{:S(2)}, u32[]{:S(2)}) async-start(bf16[16,256,128]{2,1,0:T(8,128)(2,1)} %broadcast_in_dim.9), calls=%async_computation | async-start | bytes 2097152 | tf_op jit(solution)/shard_map/all_to_all | solution.py:197
  9.7 0.8 fusion.14
  10.5 3.3 %collective-permute-start = (bf16[16,1024]{1,0:T(8,128)(2,1)S(1)}, bf16[16,1024]{1,0:T(8,128)(2,1)S(1)}, u32[]{:S(2)}, u32[]{:S(2)}) collective-permute-start(bf16[16,1024]{1,0:T(8,128)(2,1)S(1)} %get-tuple-element.14), channel_id=1, source_target_pairs={{0,16},{16,32},{32,48},{48,64},{64,80},{80,96},{96,112},{112,128},... | collective-permute-start | bytes 98312 | tf_op jit(solution)/shard_map/ppermute | solution.py:213
  13.8 1.3 %collective-permute-start.1 = (bf16[16,1024]{1,0:T(8,128)(2,1)S(1)}, bf16[16,1024]{1,0:T(8,128)(2,1)S(1)}, u32[]{:S(2)}, u32[]{:S(2)}) collective-permute-start(bf16[16,1024]{1,0:T(8,128)(2,1)S(1)} %get-tuple-element.13), channel_id=1, source_target_pairs={{16,0},{32,16},{48,32},{64,48},{80,64},{96,80},{112,96},{128,112},... | collective-permute-start | bytes 98312 | tf_op jit(solution)/shard_map/ppermute | solution.py:214
  15.1 0.7 broadcast_add_fusion
  15.8 1.5 %fusion.4 = f32[8,128]{1,0:T(8,128)S(1)} fusion(bf16[1024,8]{0,1:T(8,128)(2,1)} %param.13, bf16[1024,1024]{1,0:T(8,128)(2,1)S(1)} %copy-done, bf16[2048,1024]{1,0:T(8,128)(2,1)} %refs_2_.3, s32[]{:T(128)S(6)} %select_n.3), kind=kOutput, calls=%fused_computation.5 | convolution fusion | flops 271192064 | bytes 2379780 | tf_op jit(solution)/shard_map/dot_general | solution.py:219
  17.3 0.1 broadcast_minimum_fusion
  17.4 0.1 reshape.13
  17.5 0.6 pad.4.refs_3_.refs_5_
  18.1 3.1 %collective-permute-done.refs_4_ = bf16[16,1024]{1,0:T(8,128)(2,1)S(1)} collective-permute-done((bf16[16,1024]{1,0:T(8,128)(2,1)S(1)}, bf16[16,1024]{1,0:T(8,128)(2,1)S(1)}, u32[]{:S(2)}, u32[]{:S(2)}) %collective-permute-start) | collective-permute-done | bytes 32800 | tf_op jit(solution)/shard_map/ppermute | solution.py:213
  21.2 2.0 %collective-permute-done.1.refs_3_ = bf16[16,1024]{1,0:T(8,128)(2,1)S(1)} collective-permute-done((bf16[16,1024]{1,0:T(8,128)(2,1)S(1)}, bf16[16,1024]{1,0:T(8,128)(2,1)S(1)}, u32[]{:S(2)}, u32[]{:S(2)}) %collective-permute-start.1) | collective-permute-done | bytes 32800 | tf_op jit(solution)/shard_map/ppermute | solution.py:214
  23.2 2.6 %all-to-all-done.refs_1_ = bf16[16,256,128]{2,1,0:T(8,128)(2,1)S(1)} async-done(((bf16[16,256,128]{2,1,0:T(8,128)(2,1)}), bf16[16,256,128]{2,1,0:T(8,128)(2,1)S(1)}, u32[]{:S(2)}, u32[]{:S(2)}) %all-to-all-start) | async-done | bytes 1048608 | tf_op jit(solution)/shard_map/all_to_all | solution.py:197
  25.8 1.0 %copy-done.1 = bf16[16,256,128]{2,1,0:T(8,128)(2,1)} copy-done((bf16[16,256,128]{2,1,0:T(8,128)(2,1)}, bf16[16,256,128]{2,1,0:T(8,128)(2,1)S(1)}, u32[]{:S(2)}) %copy-start.1) | copy-done | bytes 1048600
  26.8 13.7 %row_stats.1 = f32[16,16,256]{2,1,0:T(8,128)} custom-call(s32[1]{0:T(128)} %bitcast.refs_0_, bf16[16,256,128]{2,1,0:T(8,128)(2,1)} %copy-done.1, bf16[2048,1024]{1,0:T(8,128)(2,1)} %refs_2_.3, s32[1,128]{1,0:T(1,128)} %pad.4.refs_3_.refs_5_), custom_call_target="tpu_custom_call" | custom-call | tf_op jit(solution)/shard_map/row_stats/pallas_call | solution.py:144
  40.5 5.0 %all-to-all-start.1 = ((f32[16,16,256]{2,1,0:T(8,128)}), f32[16,16,256]{2,1,0:T(8,128)S(1)}, u32[]{:S(2)}, u32[]{:S(2)}) async-start(f32[16,16,256]{2,1,0:T(8,128)} %row_stats.1), calls=%async_computation.1 | async-start | bytes 524288 | tf_op jit(solution)/shard_map/all_to_all | solution.py:224
  45.5 0.7 copy.8.refs_7_
  46.2 6.9 %all-to-all-done.1.refs_6_ = f32[16,16,256]{2,1,0:T(8,128)S(1)} async-done(((f32[16,16,256]{2,1,0:T(8,128)}), f32[16,16,256]{2,1,0:T(8,128)S(1)}, u32[]{:S(2)}, u32[]{:S(2)}) %all-to-all-start.1) | async-done | bytes 262176 | tf_op jit(solution)/shard_map/all_to_all | solution.py:224
  53.1 0.0 copy-done.3
  53.1 0.7 copy-done.2
  53.8 10.3 %key_columns.1 = f32[16,8,128]{2,1,0:T(8,128)} custom-call(s32[1]{0:T(128)} %bitcast.refs_0_, bf16[16,256,128]{2,1,0:T(8,128)(2,1)} %copy-done.1, bf16[2048,1024]{1,0:T(8,128)(2,1)} %refs_2_.3, bf16[16,1024]{1,0:T(8,128)(2,1)} %copy-done.4, bf16[16,1024]{1,0:T(8,128)(2,1)} %copy-done.3, s32[1,128]{1,0:T(1,128)} %pad.4.refs_3_.refs_5_, ...), custom_call_target="tpu_custom_call" | custom-call | tf_op jit(solution)/shard_map/key_columns/pallas_call | solution.py:168
  64.1 18.4 %all_to_all.15 = f32[16,8,128]{2,1,0:T(8,128)S(1)} all-to-all(f32[16,8,128]{2,1,0:T(8,128)} %key_columns.1), channel_id=1, replica_groups=mesh['ctx'=16,'req'=16] {'req'}, dimensions={0} | all-to-all | bytes 131072 | tf_op jit(solution)/shard_map/all_to_all | solution.py:229
  82.6 0.6 mul.25
  (11 shorter events, 0.0 us)
Async XLA Ops:
  0.0 15.8 %copy-start = (bf16[1024,1024]{1,0:T(8,128)(2,1)S(1)}, bf16[1024,1024]{1,0:T(8,128)(2,1)}, u32[]{:S(2)}) copy-start(bf16[1024,1024]{1,0:T(8,128)(2,1)} %param.12) | copy-start | bytes 6291460
  0.0 17.3 %copy-start.5 = (s32[4,16]{1,0:T(4,128)S(1)}, s32[4,16]{1,0:T(4,128)}, u32[]{:S(2)}) copy-start(s32[4,16]{1,0:T(4,128)} %param.10) | copy-start | bytes 772
  2.2 23.6 %all-to-all-start = ((bf16[16,256,128]{2,1,0:T(8,128)(2,1)}), bf16[16,256,128]{2,1,0:T(8,128)(2,1)S(1)}, u32[]{:S(2)}, u32[]{:S(2)}) async-start(bf16[16,256,128]{2,1,0:T(8,128)(2,1)} %broadcast_in_dim.9), calls=%async_computation | async-start | bytes 2097152 | tf_op jit(solution)/shard_map/all_to_all | solution.py:197
  10.5 10.7 %collective-permute-start = (bf16[16,1024]{1,0:T(8,128)(2,1)S(1)}, bf16[16,1024]{1,0:T(8,128)(2,1)S(1)}, u32[]{:S(2)}, u32[]{:S(2)}) collective-permute-start(bf16[16,1024]{1,0:T(8,128)(2,1)S(1)} %get-tuple-element.14), channel_id=1, source_target_pairs={{0,16},{16,32},{32,48},{48,64},{64,80},{80,96},{96,112},{112,128},... | collective-permute-start | bytes 98312 | tf_op jit(solution)/shard_map/ppermute | solution.py:213
  13.8 9.4 %collective-permute-start.1 = (bf16[16,1024]{1,0:T(8,128)(2,1)S(1)}, bf16[16,1024]{1,0:T(8,128)(2,1)S(1)}, u32[]{:S(2)}, u32[]{:S(2)}) collective-permute-start(bf16[16,1024]{1,0:T(8,128)(2,1)S(1)} %get-tuple-element.13), channel_id=1, source_target_pairs={{16,0},{32,16},{48,32},{64,48},{80,64},{96,80},{112,96},{128,112},... | collective-permute-start | bytes 98312 | tf_op jit(solution)/shard_map/ppermute | solution.py:214
  15.8 29.8 %copy-start.6 = (s32[8]{0:T(128)S(1)}, s32[8]{0:T(128)}, u32[]{:S(2)}) copy-start(s32[8]{0:T(128)} %param.11) | copy-start | bytes 100
  21.2 31.9 %copy-start.3 = (bf16[16,1024]{1,0:T(8,128)(2,1)}, bf16[16,1024]{1,0:T(8,128)(2,1)S(1)}, u32[]{:S(2)}) copy-start(bf16[16,1024]{1,0:T(8,128)(2,1)S(1)} %collective-permute-done.refs_4_) | copy-start | bytes 98308
  23.2 29.9 %copy-start.4 = (bf16[16,1024]{1,0:T(8,128)(2,1)}, bf16[16,1024]{1,0:T(8,128)(2,1)S(1)}, u32[]{:S(2)}) copy-start(bf16[16,1024]{1,0:T(8,128)(2,1)S(1)} %collective-permute-done.1.refs_3_) | copy-start | bytes 98308
  25.8 1.0 %copy-start.1 = (bf16[16,256,128]{2,1,0:T(8,128)(2,1)}, bf16[16,256,128]{2,1,0:T(8,128)(2,1)S(1)}, u32[]{:S(2)}) copy-start(bf16[16,256,128]{2,1,0:T(8,128)(2,1)S(1)} %all-to-all-done.refs_1_) | copy-start | bytes 3145732
  40.5 12.6 %all-to-all-start.1 = ((f32[16,16,256]{2,1,0:T(8,128)}), f32[16,16,256]{2,1,0:T(8,128)S(1)}, u32[]{:S(2)}, u32[]{:S(2)}) async-start(f32[16,16,256]{2,1,0:T(8,128)} %row_stats.1), calls=%async_computation.1 | async-start | bytes 524288 | tf_op jit(solution)/shard_map/all_to_all | solution.py:224
  53.1 0.7 copy-start.2

commit v2 on v1

v2 whole, which is shorter than its diff:
```python
import math

import jax
import jax.numpy as jnp
from jax import lax
from jax.experimental import pallas as pl
from jax.experimental.pallas import tpu as pltpu
from jax.sharding import PartitionSpec as P


RAD = 3
MASKED = -1e30
LOG2E = 1.4426950408889634
HALO = 128
EDGE = 16
HEADS_STEP = 2
SAMPLE = 64
LARGE = 2.0**100
NT = (((1,), (1,)), ((), ()))


def penalty_rows(first_key, count, limits, is_halo, key_total, key_dev):
    local = lax.broadcasted_iota(jnp.int32, (count, 128), 0)
    if is_halo:
        after = local < HALO // 2
        key = jnp.where(after, first_key + key_dev + local, first_key - HALO + local)
        real = ((local < RAD) | (local >= HALO - RAD)) & (key >= 0) & (key < key_total)
        return jnp.where(real & (key <= limits), 0.0, MASKED).astype(jnp.bfloat16)
    return jnp.where(first_key + local <= limits, 0.0, MASKED).astype(jnp.bfloat16)


def one_hot_rows(chunk_rows, heads):
    row = lax.broadcasted_iota(jnp.int32, (chunk_rows, 128), 0)
    lane = lax.broadcasted_iota(jnp.int32, (chunk_rows, 128), 1)
    low = lane * heads
    return jnp.where((row >= low) & (row < low + heads), 1.0, 0.0).astype(jnp.bfloat16)


def stats_kernel(first_ref, q_ref, k_ref, lim_ref, out_ref, pen, hot, lse, totals, *, heads, scale2):
    step = pl.program_id(0)
    group, chunk_rows, head_dim = q_ref.shape
    key_dev = k_ref.shape[0]
    per = group * head_dim // k_ref.shape[1]
    block = 256

    @pl.when(step == 0)
    def _():
        for b in range(key_dev // block):
            pen[b * block : (b + 1) * block] = penalty_rows(
                first_ref[0] + b * block, block, lim_ref[...], False, 0, 0
            )
        hot[...] = one_hot_rows(chunk_rows, heads)

    def scored(chunk):
        v = chunk // per
        keys = jnp.concatenate([k_ref[:, v * head_dim : (v + 1) * head_dim], pen[...]], axis=1)
        rows = jnp.concatenate([q_ref[chunk], hot[...]], axis=1)
        return lax.dot_general(keys, rows, NT, preferred_element_type=jnp.float32)

    for chunk in range(group):
        s = scored(chunk)
        base = jnp.max(s[:SAMPLE], axis=0, keepdims=True)
        total = jnp.sum(jnp.exp2((s - base) * scale2), axis=0, keepdims=True)
        lse[pl.ds(step * group + chunk, 1), :] = base * scale2 + jnp.log2(total)
        totals[chunk : chunk + 1] = total

    @pl.when(jnp.logical_not(jnp.max(totals[...]) < LARGE))
    def _():
        for chunk in range(group):
            s = scored(chunk)
            top = jnp.max(s, axis=0, keepdims=True)
            total = jnp.sum(jnp.exp2((s - top) * scale2), axis=0, keepdims=True)
            lse[pl.ds(step * group + chunk, 1), :] = top * scale2 + jnp.log2(total)

    @pl.when(step == pl.num_programs(0) - 1)
    def _():
        everything = lse[...]
        for i in range(out_ref.shape[0]):
            out_ref[i] = everything


def to_column(row):
    r = lax.broadcasted_iota(jnp.int32, (128, 128), 0)
    c = lax.broadcasted_iota(jnp.int32, (128, 128), 1)
    return jnp.sum(jnp.where(r == c, row, 0.0), axis=1, keepdims=True)


def columns_kernel(
    first_ref, q_ref, k_ref, next_ref, prev_ref, lim_ref, parts_ref, width_ref, out_ref,
    pen, hot, lse, cols, *, heads, scale2, key_total,
):
    step = pl.program_id(0)
    group, chunk_rows, head_dim = q_ref.shape
    key_dev = k_ref.shape[0]
    heads_here = k_ref.shape[1] // head_dim
    per = group // heads_here
    block = 256

    @pl.when(step == 0)
    def _():
        for b in range(key_dev // block):
            pen[b * block : (b + 1) * block] = penalty_rows(
                first_ref[0] + b * block, block, lim_ref[...], False, 0, 0
            )
        pen[key_dev:] = penalty_rows(first_ref[0], HALO, lim_ref[...], True, key_total, key_dev)
        hot[...] = one_hot_rows(chunk_rows, heads)
        peers = parts_ref.shape[0]
        top = parts_ref[0]
        for i in range(1, peers):
            top = jnp.maximum(top, parts_ref[i])
        total = jnp.exp2(parts_ref[0] - top)
        for i in range(1, peers):
            total = total + jnp.exp2(parts_ref[i] - top)
        lse[...] = top + jnp.log2(total)

    for h in range(heads_here):
        lanes = slice(h * head_dim, (h + 1) * head_dim)
        columns = []
        for p in range(per):
            row = lse[pl.ds(step * group + h * per + p, 1), :]
            for j in range(chunk_rows // 128):
                columns.append(to_column(row[:, j * 128 : (j + 1) * 128]))
        shift = jnp.concatenate(columns, axis=0)
        rows = jnp.concatenate(
            [jnp.concatenate([q_ref[h * per + p], hot[...]], axis=1) for p in range(per)], axis=0
        )
        gap = jnp.zeros((HALO - 2 * EDGE, head_dim), jnp.bfloat16)
        edges = jnp.concatenate([next_ref[:, lanes], gap, prev_ref[:, lanes]], axis=0)
        start = 0
        while start < key_dev + HALO:
            size = min(block, key_dev + HALO - start)
            some = edges if start >= key_dev else k_ref[start : start + size, lanes]
            keys = jnp.concatenate([some, pen[start : start + size]], axis=1)
            s = lax.dot_general(rows, keys, NT, preferred_element_type=jnp.float32)
            weights = jnp.exp2(s * scale2 - shift)
            cols[step * heads_here + h, :, start : start + size] = jnp.sum(weights.reshape(-1, 8, size), axis=0)
            start += size

    @pl.when(step == pl.num_programs(0) - 1)
    def _():
        width = width_ref[...]
        below = width // 2
        above = (width - 1) // 2
        whole = jnp.sum(cols[...], axis=1)
        length = whole.shape[1]
        pooled = jnp.where(above >= 0, whole, 0.0)
        for tap in range(1, RAD + 1):
            pooled = pooled + jnp.where(tap <= above, pltpu.roll(whole, length - tap, 1), 0.0)
            pooled = pooled + jnp.where(tap <= below, pltpu.roll(whole, tap, 1), 0.0)
        pooled = pooled / width.astype(jnp.float32)
        piece = key_dev // out_ref.shape[0]
        for i in range(out_ref.shape[0]):
            out_ref[i] = pooled[:, i * piece : (i + 1) * piece]


def row_stats(first, chunks, keys, lim, key_heads, heads, scale2):
    n, chunk_rows, head_dim = chunks.shape
    key_dev = keys.shape[0]
    steps = key_heads // HEADS_STEP
    group = n // steps
    width = HEADS_STEP * head_dim
    return pl.pallas_call(
        lambda *refs: stats_kernel(*refs, heads=heads, scale2=scale2),
        out_shape=jax.ShapeDtypeStruct((n, n, chunk_rows), jnp.float32),
        grid=(steps,),
        in_specs=[
            pl.BlockSpec(memory_space=pltpu.SMEM),
            pl.BlockSpec((group, chunk_rows, head_dim), lambda i: (i, 0, 0)),
            pl.BlockSpec((key_dev, width), lambda i: (0, i)),
            pl.BlockSpec((1, 128), lambda i: (0, 0)),
        ],
        out_specs=pl.BlockSpec((n, n, chunk_rows), lambda i: (0, 0, 0)),
        scratch_shapes=[
            pltpu.VMEM((key_dev, 128), jnp.bfloat16),
            pltpu.VMEM((chunk_rows, 128), jnp.bfloat16),
            pltpu.VMEM((n, chunk_rows), jnp.float32),
            pltpu.VMEM((group, chunk_rows), jnp.float32),
        ],
        name="row_stats",
    )(first, chunks, keys, lim)


def key_columns(first, chunks, keys, after, before, lim, parts, width, key_heads, heads, scale2, key_total, owners):
    n, chunk_rows, head_dim = chunks.shape
    key_dev = keys.shape[0]
    steps = key_heads // HEADS_STEP
    group = n // steps
    wide = HEADS_STEP * head_dim
    return pl.pallas_call(
        lambda *refs: columns_kernel(*refs, heads=heads, scale2=scale2, key_total=key_total),
        out_shape=jax.ShapeDtypeStruct((owners, key_heads, key_dev // owners), jnp.float32),
        grid=(steps,),
        in_specs=[
            pl.BlockSpec(memory_space=pltpu.SMEM),
            pl.BlockSpec((group, chunk_rows, head_dim), lambda i: (i, 0, 0)),
            pl.BlockSpec((key_dev, wide), lambda i: (0, i)),
            pl.BlockSpec((EDGE, wide), lambda i: (0, i)),
            pl.BlockSpec((EDGE, wide), lambda i: (0, i)),
            pl.BlockSpec((1, 128), lambda i: (0, 0)),
            pl.BlockSpec((n, n, chunk_rows), lambda i: (0, 0, 0)),
            pl.BlockSpec((key_heads, 1), lambda i: (0, 0)),
        ],
        out_specs=pl.BlockSpec((owners, key_heads, key_dev // owners), lambda i: (0, 0, 0)),
        scratch_shapes=[
            pltpu.VMEM((key_dev + HALO, 128), jnp.bfloat16),
            pltpu.VMEM((chunk_rows, 128), jnp.bfloat16),
            pltpu.VMEM((n, chunk_rows), jnp.float32),
            pltpu.VMEM((key_heads, 8, key_dev + HALO), jnp.float32),
        ],
        name="key_columns",
    )(first, chunks, keys, after, before, lim, parts, width)


def sent_to_all(array, axis):
    length = lax.axis_size(axis)
    return lax.all_to_all(jnp.broadcast_to(array[None], (length, *array.shape)), axis, 0, 0, tiled=True)


def per_device(queries, prefix_keys, lengths, positions, pool_width, scorer_in, scorer_out):
    row_count, heads, head_dim = queries.shape
    key_heads = pool_width.shape[0]
    key_dev = prefix_keys.shape[0]
    shards = lax.axis_size("ctx")
    owners = lax.axis_size("req")
    scale2 = LOG2E / math.sqrt(head_dim)
    limits = jnp.minimum(positions, lengths[:, None] - 1).reshape(1, row_count)
    lim = jnp.pad(limits, ((0, 0), (0, 128 - row_count)), constant_values=2**30)
    first = (lax.axis_index("ctx") * key_dev).reshape(1).astype(jnp.int32)
    up = [(i, i + 1) for i in range(shards - 1)]
    chunks = sent_to_all(queries.reshape(row_count * heads, head_dim), "ctx")
    chunks = chunks.reshape(shards, row_count * heads, head_dim)
    before = lax.ppermute(prefix_keys[key_dev - EDGE :], "ctx", up)
    after = lax.ppermute(prefix_keys[:EDGE], "ctx", [(b, a) for a, b in up])

    owned = key_dev // owners
    owned_keys = lax.dynamic_slice_in_dim(prefix_keys, lax.axis_index("req") * owned, owned, 0)
    hidden = jax.nn.silu(jnp.dot(owned_keys, scorer_in, preferred_element_type=jnp.float32)).astype(jnp.bfloat16)
    gating = jnp.dot(hidden, scorer_out, preferred_element_type=jnp.float32)
    gate = (2.0 * jax.nn.sigmoid(gating)).T
    chunks, gate = lax.optimization_barrier((chunks, gate))
    chunks = pltpu.with_memory_space_constraint(chunks, pltpu.VMEM)

    local = row_stats(first, chunks, prefix_keys, lim, key_heads, heads, scale2)
    parts = lax.all_to_all(local, "ctx", 0, 0, tiled=True)
    parts = pltpu.with_memory_space_constraint(parts, pltpu.VMEM)
    pooled = key_columns(
        first, chunks, prefix_keys, after, before, lim, parts, pool_width.reshape(key_heads, 1),
        key_heads, heads, scale2, shards * key_dev, owners,
    )
    pieces = lax.all_to_all(pooled, "req", 0, 0, tiled=True)
    return jnp.sum(pieces, axis=0) * gate


def solution(mesh):
    placed = (P("req", "ctx", None), P("ctx", None), P("req"), P("req", None), P(), P(), P())

    return jax.shard_map(per_device, mesh=mesh, in_specs=placed, out_specs=P(None, ("ctx", "req")), check_vma=False)
```

time: 83.8 us -> 89.2 us (1.064)
  the two profiles are of different devices: /device:TPU:1 before, /device:TPU:25 now
where the time goes in v2:
time: 89.2 us; the launch traced here: 88.6 us
  starting transfers between devices  27.8 us (31%)
  blocking collectives  21.2 us (24%)
  Pallas kernels  16.6 us (19%)
  waiting for transfers between devices  14.6 us (16%)
  local copies, waits for them, and re-layouts  4.86 us (5%)
  other arithmetic  2.02 us (2%)
  matrix products  1.55 us (2%)
    all_to_all x1, blocking collectives, per_device(): pieces = lax.all_to_all(pooled, 'req', 0, 0, tiled=True)  21.2 us
    all_to_all x1, starting transfers between devices, per_device(): parts = lax.all_to_all(local, 'ctx', 0, 0, tiled=True)  14.7 us
    all_to_all x1, waiting for transfers between devices, sent_to_all(): lax.all_to_all(jnp.broadcast_to(array[None], (length, *array.shape)), axi...  10.4 us
    pallas_call x1, Pallas kernels, key_columns(): pl.pallas_call(lambda *refs: columns_kernel(*refs, heads=heads, scale2=sc...  8.57 us
    pallas_call x1, Pallas kernels, row_stats(): pl.pallas_call(lambda *refs: stats_kernel(*refs, heads=heads, scale2=scal...  8.05 us
    all_to_all x1, starting transfers between devices, sent_to_all(): lax.all_to_all(jnp.broadcast_to(array[None], (length, *array.shape)), axi...  6.61 us
    ppermute x1, starting transfers between devices, per_device(): after = lax.ppermute(prefix_keys[:EDGE], 'ctx', [(b, a) for a, b in up])  4.58 us
    ppermute x1, waiting for transfers between devices, per_device(): before = lax.ppermute(prefix_keys[key_dev - EDGE:], 'ctx', up)  4.15 us
  transfers between devices with their start and end apart: 4, of which 2 were waited for; matrix products, arithmetic and copies ran while one was open for 6% of the time, Pallas kernels for 0%

profile of v2, /device:TPU:25, one launch (start us, length us, event | category | flops | bytes accessed | tf_op | source)
XLA Modules:
  0.0 88.6 jit_solution(18158910226347420849)
XLA Ops:
  0.0 0.0 copy-start
  0.0 2.2 %broadcast_in_dim.9 = bf16[16,256,128]{2,1,0:T(8,128)(2,1)} broadcast(bf16[256,128]{1,0:T(8,128)(2,1)} %bitcast.7), dimensions={1,2} | broadcast | bytes 1114112 | tf_op jit(solution)/shard_map/broadcast_in_dim | solution.py:216
  2.2 6.6 %all-to-all-start = ((bf16[16,256,128]{2,1,0:T(8,128)(2,1)}), bf16[16,256,128]{2,1,0:T(8,128)(2,1)S(1)}, u32[]{:S(2)}, u32[]{:S(2)}) async-start(bf16[16,256,128]{2,1,0:T(8,128)(2,1)} %broadcast_in_dim.9), calls=%async_computation | async-start | bytes 2097152 | tf_op jit(solution)/shard_map/all_to_all | solution.py:216
  8.8 0.7 broadcast_add_fusion
  9.4 0.8 broadcast_minimum_fusion
  10.2 0.1 reshape.13
  10.3 0.5 pad.4.refs_3_.refs_5_
  10.8 0.0 copy-done
  10.8 1.5 %fusion.4 = f32[8,128]{1,0:T(8,128)S(1)} fusion(bf16[1024,8]{0,1:T(8,128)(2,1)} %param.13, bf16[1024,1024]{1,0:T(8,128)(2,1)S(1)} %copy-done, bf16[2048,1024]{1,0:T(8,128)(2,1)} %refs_2_.3, s32[]{:T(128)S(6)} %select_n.3), kind=kOutput, calls=%fused_computation.5 | convolution fusion | flops 271192064 | bytes 2379780 | tf_op jit(solution)/shard_map/dot_general | solution.py:238
  12.4 10.4 %all-to-all-done.refs_1_ = bf16[16,256,128]{2,1,0:T(8,128)(2,1)S(1)} async-done(((bf16[16,256,128]{2,1,0:T(8,128)(2,1)}), bf16[16,256,128]{2,1,0:T(8,128)(2,1)S(1)}, u32[]{:S(2)}, u32[]{:S(2)}) %all-to-all-start) | async-done | bytes 1048608 | tf_op jit(solution)/shard_map/all_to_all | solution.py:216
  22.8 8.0 %row_stats.1 = f32[16,16,256]{2,1,0:T(8,128)} custom-call(s32[1]{0:T(128)} %bitcast.refs_0_, bf16[16,256,128]{2,1,0:T(8,128)(2,1)S(1)} %all-to-all-done.refs_1_, bf16[2048,1024]{1,0:T(8,128)(2,1)} %refs_2_.3, s32[1,128]{1,0:T(1,128)} %pad.4.refs_3_.refs_5_), custom_call_target="tpu_custom_call" | custom-call | tf_op jit(solution)/shard_map/row_stats/pallas_call | solution.py:162
  30.9 14.7 %all-to-all-start.1 = ((f32[16,16,256]{2,1,0:T(8,128)}), f32[16,16,256]{2,1,0:T(8,128)S(1)}, u32[]{:S(2)}, u32[]{:S(2)}) async-start(f32[16,16,256]{2,1,0:T(8,128)} %row_stats.1), calls=%async_computation.1 | async-start | bytes 524288 | tf_op jit(solution)/shard_map/all_to_all | solution.py:244
  45.5 0.8 fusion.14
  46.3 4.6 %collective-permute-start = (bf16[16,1024]{1,0:T(8,128)(2,1)S(1)}, bf16[16,1024]{1,0:T(8,128)(2,1)S(1)}, u32[]{:S(2)}, u32[]{:S(2)}) collective-permute-start(bf16[16,1024]{1,0:T(8,128)(2,1)S(1)} %get-tuple-element.10), channel_id=1, source_target_pairs={{16,0},{32,16},{48,32},{64,48},{80,64},{96,80},{112,96},{128,112},... | collective-permute-start | bytes 98312 | tf_op jit(solution)/shard_map/ppermute | solution.py:233
  50.9 1.9 %collective-permute-start.1 = (bf16[16,1024]{1,0:T(8,128)(2,1)S(1)}, bf16[16,1024]{1,0:T(8,128)(2,1)S(1)}, u32[]{:S(2)}, u32[]{:S(2)}) collective-permute-start(bf16[16,1024]{1,0:T(8,128)(2,1)S(1)} %get-tuple-element.9), channel_id=1, source_target_pairs={{0,16},{16,32},{32,48},{48,64},{64,80},{80,96},{96,112},{112,128},... | collective-permute-start | bytes 98312 | tf_op jit(solution)/shard_map/ppermute | solution.py:232
  52.8 0.0 copy-done.3
  52.8 0.7 copy.8.refs_7_
  53.5 0.0 collective-permute-done.refs_3_
  53.5 4.2 %collective-permute-done.1.refs_4_ = bf16[16,1024]{1,0:T(8,128)(2,1)S(1)} collective-permute-done((bf16[16,1024]{1,0:T(8,128)(2,1)S(1)}, bf16[16,1024]{1,0:T(8,128)(2,1)S(1)}, u32[]{:S(2)}, u32[]{:S(2)}) %collective-permute-start.1) | collective-permute-done | bytes 32800 | tf_op jit(solution)/shard_map/ppermute | solution.py:232
  57.7 0.0 all-to-all-done.1.refs_6_
  57.7 0.6 copy-done.2
  58.3 8.6 %key_columns.1 = f32[16,8,128]{2,1,0:T(8,128)} custom-call(s32[1]{0:T(128)} %bitcast.refs_0_, bf16[16,256,128]{2,1,0:T(8,128)(2,1)S(1)} %all-to-all-done.refs_1_, bf16[2048,1024]{1,0:T(8,128)(2,1)} %refs_2_.3, bf16[16,1024]{1,0:T(8,128)(2,1)} %copy-done.1, bf16[16,1024]{1,0:T(8,128)(2,1)} %copy-done.2, s32[1,128]{1,0:T(1,128)} %pad.4.refs_3_.refs_5_, ...), custom_call_target="tpu_custom_call" | custom-call | tf_op jit(solution)/shard_map/key_columns/pallas_call | solution.py:189
  66.9 21.2 %all_to_all.15 = f32[16,8,128]{2,1,0:T(8,128)S(1)} all-to-all(f32[16,8,128]{2,1,0:T(8,128)} %key_columns.1), channel_id=1, replica_groups=mesh['ctx'=16,'req'=16] {'req'}, dimensions={0} | all-to-all | bytes 131072 | tf_op jit(solution)/shard_map/all_to_all | solution.py:250
  88.0 0.6 mul.25
  (5 shorter events, 0.0 us)
Async XLA Ops:
  0.0 10.8 %copy-start = (bf16[1024,1024]{1,0:T(8,128)(2,1)S(1)}, bf16[1024,1024]{1,0:T(8,128)(2,1)}, u32[]{:S(2)}) copy-start(bf16[1024,1024]{1,0:T(8,128)(2,1)} %param.12) | copy-start | bytes 6291460
  2.2 20.6 %all-to-all-start = ((bf16[16,256,128]{2,1,0:T(8,128)(2,1)}), bf16[16,256,128]{2,1,0:T(8,128)(2,1)S(1)}, u32[]{:S(2)}, u32[]{:S(2)}) async-start(bf16[16,256,128]{2,1,0:T(8,128)(2,1)} %broadcast_in_dim.9), calls=%async_computation | async-start | bytes 2097152 | tf_op jit(solution)/shard_map/all_to_all | solution.py:216
  10.8 42.0 %copy-start.3 = (s32[8]{0:T(128)S(1)}, s32[8]{0:T(128)}, u32[]{:S(2)}) copy-start(s32[8]{0:T(128)} %param.11) | copy-start | bytes 100
  30.9 26.8 %all-to-all-start.1 = ((f32[16,16,256]{2,1,0:T(8,128)}), f32[16,16,256]{2,1,0:T(8,128)S(1)}, u32[]{:S(2)}, u32[]{:S(2)}) async-start(f32[16,16,256]{2,1,0:T(8,128)} %row_stats.1), calls=%async_computation.1 | async-start | bytes 524288 | tf_op jit(solution)/shard_map/all_to_all | solution.py:244
  46.3 7.2 %collective-permute-start = (bf16[16,1024]{1,0:T(8,128)(2,1)S(1)}, bf16[16,1024]{1,0:T(8,128)(2,1)S(1)}, u32[]{:S(2)}, u32[]{:S(2)}) collective-permute-start(bf16[16,1024]{1,0:T(8,128)(2,1)S(1)} %get-tuple-element.10), channel_id=1, source_target_pairs={{16,0},{32,16},{48,32},{64,48},{80,64},{96,80},{112,96},{128,112},... | collective-permute-start | bytes 98312 | tf_op jit(solution)/shard_map/ppermute | solution.py:233
  50.9 6.8 %collective-permute-start.1 = (bf16[16,1024]{1,0:T(8,128)(2,1)S(1)}, bf16[16,1024]{1,0:T(8,128)(2,1)S(1)}, u32[]{:S(2)}, u32[]{:S(2)}) collective-permute-start(bf16[16,1024]{1,0:T(8,128)(2,1)S(1)} %get-tuple-element.9), channel_id=1, source_target_pairs={{0,16},{16,32},{32,48},{48,64},{64,80},{80,96},{96,112},{112,128},... | collective-permute-start | bytes 98312 | tf_op jit(solution)/shard_map/ppermute | solution.py:232
  53.5 4.2 %copy-start.1 = (bf16[16,1024]{1,0:T(8,128)(2,1)}, bf16[16,1024]{1,0:T(8,128)(2,1)S(1)}, u32[]{:S(2)}) copy-start(bf16[16,1024]{1,0:T(8,128)(2,1)S(1)} %collective-permute-done.refs_3_) | copy-start | bytes 98308
  57.7 0.6 copy-start.2
